TPU v7x, 32 devices: a whole 2x2x4 slice. The times are simulated.
32 devices in a mesh: dp: 2 (over y), seq: 8 (over z, x), head: 2 (over core).
Axes of the slice: x: 2, y: 2, z: 4, core: 2. Of those that a mesh axis runs over, the one named last changes fastest.
Arguments:
- tokens: bfloat16 [2, 2, 1024, 2048], P(None, 'dp', 'seq'), may hold values from -6 to 6
- norm_gain: float32 [2048], replicated, may hold values from 0.5 to 1.5
- w_gate_in: bfloat16 [2048, 4096], P(('dp', 'seq'), 'head'), may hold values from -0.125 to 0.125
- w_x_in: bfloat16 [2048, 4096], P(('dp', 'seq'), 'head'), may hold values from -0.125 to 0.125
- w_bc_in: bfloat16 [2048, 256], P(('dp', 'seq')), may hold values from -0.125 to 0.125
- w_dt_in: bfloat16 [2048, 64], P(('dp', 'seq'), 'head'), may hold values from -0.0625 to 0.0625
- conv_x_w: float32 [4, 4096], P(None, 'head'), may hold values from -3 to 3
- conv_x_b: float32 [4096], P('head'), may hold values from -3 to 3
- conv_bc_w: float32 [4, 256], replicated, may hold values from -3 to 3
- conv_bc_b: float32 [256], replicated, may hold values from -3 to 3
- dt_bias: float32 [64], P('head'), may hold values from -7 to -2
- a_log: float32 [64], P('head'), may hold values from 0 to 1.5
- d_skip: float32 [64], P('head'), may hold values from 0.5 to 1.5
- gate_gain: float32 [4096], P('head'), may hold values from 0.5 to 1.5
- w_out: bfloat16 [4096, 2048], P('head', ('dp', 'seq')), may hold values from -0.09375 to 0.09375
- prefix_len: int32 [2, 2], P(None, 'dp'), may hold values from 102 to 1024, as said below
- cotangent: bfloat16 [2, 2, 1024, 2048], P(None, 'dp', 'seq'), may hold values from -6 to 6
Outputs:
- result: bfloat16 [2, 2, 1024, 2048], P(None, 'dp', 'seq')
- grad_tokens: float32 [2, 2, 1024, 2048], P(None, 'dp', 'seq')
- grad_norm_gain: float32 [2048], replicated
- grad_w_gate_in: float32 [2048, 4096], P(('dp', 'seq'), 'head')
- grad_w_x_in: float32 [2048, 4096], P(('dp', 'seq'), 'head')
- grad_w_bc_in: float32 [2048, 256], P(('dp', 'seq'))
- grad_w_dt_in: float32 [2048, 64], P(('dp', 'seq'), 'head')
- grad_conv_x_w: float32 [4, 4096], P(None, 'head')
- grad_conv_x_b: float32 [4096], P('head')
- grad_conv_bc_w: float32 [4, 256], replicated
- grad_conv_bc_b: float32 [256], replicated
- grad_dt_bias: float32 [64], P('head')
- grad_a_log: float32 [64], P('head')
- grad_d_skip: float32 [64], P('head')
- grad_gate_gain: float32 [4096], P('head')
- grad_w_out: float32 [4096, 2048], P('head', ('dp', 'seq'))
Inputs may be any that keep to these rules, and one draw needn't show every extreme that they name: Tokens before a sequence's prefix_len mix both ways; some sequence has exactly 1024 and some exactly 102.
All inputs are finite; a program needn't handle non-finite values.
Results may differ from a plain program's by a relative error of at most 0.012.
Values may be sent and summed in bfloat16 or wider, within the bound.
A program may use at most 256 MiB of HBM per device.

v0:
```python
import jax
import jax.numpy as jnp
from jax import lax
from jax.sharding import PartitionSpec as P

EPSILON = 1e-05
HIGHEST = lax.Precision.HIGHEST
BF16 = jnp.bfloat16
F32 = jnp.float32
CHUNK = 128


def dot_f32(a, b):
    return jnp.dot(a, b, preferred_element_type=F32)


def causal_conv(signal, kernel, bias):
    margin = kernel.shape[0] - 1
    length = signal.shape[1]
    padded = jnp.pad(signal, ((0, 0), (margin, 0), (0, 0)))
    summed = bias + jnp.zeros_like(signal)
    for offset in range(kernel.shape[0]):
        summed = summed + kernel[offset] * padded[:, offset : offset + length]
    return summed


def mixer(
    prefix, inner, bc, dt_raw, conv_x_w, conv_x_b, conv_bc_w, conv_bc_b, dt_bias, a_log, d_skip
):
    seqs, length, width = inner.shape
    heads = dt_raw.shape[-1]
    state = bc.shape[-1] // 2
    chunk = CHUNK
    count = length // chunk
    values = jax.nn.silu(causal_conv(inner, conv_x_w, conv_x_b))
    active = jax.nn.silu(causal_conv(bc, conv_bc_w, conv_bc_b))
    values = values.reshape(seqs, count, chunk, heads, width // heads)
    b_in = active[..., :state].reshape(seqs, count, chunk, state)
    c_out = active[..., state:].reshape(seqs, count, chunk, state)
    dt = jax.nn.softplus(dt_raw + dt_bias).reshape(seqs, count, chunk, heads)
    cum = jnp.cumsum(dt * -jnp.exp(a_log), axis=2)
    end = cum[:, :, -1:, :]
    places = jnp.arange(length, dtype=jnp.int32).reshape(count, chunk)
    inside = (places[None] < prefix[:, None, None])[..., None]
    weighted = values * dt[..., None]
    ends_state = jnp.einsum(
        "skth,skthp,sktn->skhpn", jnp.exp(end - cum), weighted, b_in, precision=HIGHEST
    )
    back_state = jnp.einsum(
        "skth,skthp,sktn->skhpn",
        jnp.where(inside, jnp.exp(cum), 0.0),
        weighted,
        b_in,
        precision=HIGHEST,
    )
    decay = jnp.exp(end[:, :, 0])[..., None, None]
    zero = jnp.zeros_like(ends_state[:, 0])
    state_in, back_in = ([zero], [zero])
    for k in range(count - 1):
        state_in.append(state_in[-1] * decay[:, k] + ends_state[:, k])
        back_in.append(back_in[-1] * decay[:, count - 1 - k] + back_state[:, count - 1 - k])
    state_in = jnp.stack(state_in, axis=1)
    back_in = jnp.stack(back_in[::-1], axis=1)
    scores = jnp.einsum("sktn,skun->sktu", c_out, b_in, precision=HIGHEST)
    spread = cum[:, :, :, None, :] - cum[:, :, None, :, :]
    behind = (places[:, :, None] >= places[:, None, :])[None, ..., None]
    ahead = (
        (places[:, :, None] < places[:, None, :])[None]
        & (places[None, :, None, :] < prefix[:, None, None, None])
    )[..., None]
    masked = jnp.where(behind, jnp.exp(jnp.where(behind, spread, 0.0)), 0.0) + jnp.where(
        ahead, jnp.exp(jnp.where(ahead, -spread, 0.0)), 0.0
    )
    out = jnp.einsum("sktuh,skuhp->skthp", scores[..., None] * masked, weighted, precision=HIGHEST)
    out = out + jnp.exp(cum)[..., None] * jnp.einsum(
        "sktn,skhpn->skthp", c_out, state_in, precision=HIGHEST
    )
    out = out + jnp.exp(end - cum)[..., None] * jnp.einsum(
        "sktn,skhpn->skthp", c_out, back_in, precision=HIGHEST
    )
    out = out + d_skip[:, None] * values
    return out.reshape(seqs, length, width)


def body(
    tokens,
    norm_gain,
    w_gate_in,
    w_x_in,
    w_bc_in,
    w_dt_in,
    conv_x_w,
    conv_x_b,
    conv_bc_w,
    conv_bc_b,
    dt_bias,
    a_log,
    d_skip,
    gate_gain,
    w_out,
    prefix_len,
    cotangent,
):
    dp, sq, hd = (lax.axis_size("dp"), lax.axis_size("seq"), lax.axis_size("head"))
    me_seq, me_head = (lax.axis_index("seq"), lax.axis_index("head"))
    micro, seqs, span, model = tokens.shape
    group = micro * seqs
    length = span * sq
    rows_here = group * span
    own_rows = rows_here // hd
    half = w_x_in.shape[1]
    width = half // sq
    heads = w_dt_in.shape[1] // sq
    full_inner = half * hd
    prefix = prefix_len.reshape(group)
    everyone = ("seq", "head")

    def mine(x):
        return lax.dynamic_slice_in_dim(
            x.reshape(rows_here, model), me_head * own_rows, own_rows, 0
        )

    def to_sequences(x):
        return x.reshape(sq, group, span, -1).transpose(1, 0, 2, 3).reshape(group, length, -1)

    def from_sequences(x):
        return x.reshape(group, sq, span, -1).transpose(1, 0, 2, 3).reshape(sq * rows_here, -1)

    def rms(x, gain):
        return x * lax.rsqrt(jnp.mean(x * x, axis=-1, keepdims=True) + EPSILON) * gain

    my_tokens = mine(tokens).astype(F32)
    my_cot = mine(cotangent)
    normed_own = rms(my_tokens, norm_gain).astype(BF16)
    normed = lax.all_gather(normed_own, everyone, axis=0, tiled=True)

    def columns(w):
        return lax.all_gather(
            lax.all_to_all(w, "seq", split_axis=1, concat_axis=0, tiled=True),
            "dp",
            axis=0,
            tiled=True,
        )

    wg = columns(w_gate_in)
    wx = columns(w_x_in)
    wd = lax.dynamic_slice_in_dim(
        lax.all_gather(w_dt_in, ("dp", "seq"), axis=0, tiled=True), me_seq * heads, heads, 1
    )
    wb = lax.all_gather(w_bc_in, ("dp", "seq"), axis=0, tiled=True)
    wo = lax.all_gather(
        lax.all_to_all(w_out, "seq", split_axis=0, concat_axis=1, tiled=True),
        "dp",
        axis=1,
        tiled=True,
    )
    cot = lax.all_gather(my_cot, everyone, axis=0, tiled=True)

    def part(x, size, axis):
        return lax.dynamic_slice_in_dim(x, me_seq * size, size, axis)

    cxw, cxb = (part(conv_x_w, width, 1), part(conv_x_b, width, 0))
    dtb, alog, dsk = (part(dt_bias, heads, 0), part(a_log, heads, 0), part(d_skip, heads, 0))
    gain = part(gate_gain, width, 0)

    def project(w):
        return to_sequences(dot_f32(normed, w).astype(BF16)).astype(F32)

    gate, inner, bc, dt_raw = (project(wg), project(wx), project(wb), project(wd))
    mixed, pull = jax.vjp(
        lambda *a: mixer(prefix, *a),
        inner,
        bc,
        dt_raw,
        cxw,
        cxb,
        conv_bc_w,
        conv_bc_b,
        dtb,
        alog,
        dsk,
    )
    sig = jax.nn.sigmoid(gate)
    act = gate * sig
    gated = mixed * act
    grad_scaled = to_sequences(jnp.einsum("rd,kd->rk", cot, wo, preferred_element_type=F32))
    gs = grad_scaled * gain
    sums = lax.psum(
        jnp.stack([jnp.sum(gated * gated, axis=-1), jnp.sum(gs * gated, axis=-1)]), everyone
    )
    scale = lax.rsqrt(sums[0][..., None] / full_inner + EPSILON)
    unit = gated * scale
    scaled = from_sequences((unit * gain).astype(BF16))
    branch = lax.psum_scatter(
        dot_f32(scaled, wo).astype(BF16), everyone, scatter_dimension=0, tiled=True
    )
    result_own = (my_tokens + branch.astype(F32)).astype(BF16)
    grad_gain = jnp.sum(grad_scaled * unit, axis=(0, 1))
    grad_wo = jnp.einsum("rk,rd->kd", scaled, cot, preferred_element_type=F32)
    grad_gated = gs * scale - gated * (scale * scale * scale * (sums[1][..., None] / full_inner))
    grad_mixed = grad_gated * act
    grad_gate = grad_gated * mixed * (sig * (1.0 + gate * (1.0 - sig)))
    d_inner, d_bc, d_dt, d_cxw, d_cxb, d_cbw, d_cbb, d_dtb, d_alog, d_dsk = pull(grad_mixed)
    gg = from_sequences(grad_gate.astype(BF16))
    gx = from_sequences(d_inner.astype(BF16))
    gd = from_sequences(d_dt.astype(BF16))
    gb_own = lax.psum_scatter(
        from_sequences(d_bc), everyone, scatter_dimension=0, tiled=True
    ).astype(BF16)

    def inward(g, w):
        return jnp.einsum("rc,kc->rk", g, w, preferred_element_type=F32)

    def weight_grad(n, g):
        return jnp.einsum("rk,rc->kc", n, g, preferred_element_type=F32)

    part_normed = inward(gg, wg) + inward(gx, wx) + inward(gd, wd)
    grad_normed = lax.psum_scatter(
        part_normed.astype(BF16), everyone, scatter_dimension=0, tiled=True
    ).astype(F32) + inward(gb_own, wb)
    _, pull_norm = jax.vjp(rms, my_tokens, norm_gain)
    grad_rows, grad_norm = pull_norm(grad_normed)
    grad_own = my_cot.astype(F32) + grad_rows

    def home(g):
        return lax.all_to_all(
            lax.psum_scatter(g.astype(BF16), "dp", scatter_dimension=0, tiled=True),
            "seq",
            split_axis=0,
            concat_axis=1,
            tiled=True,
        ).astype(F32)

    g_gate, g_x = (home(weight_grad(normed, gg)), home(weight_grad(normed, gx)))
    g_dt = lax.all_to_all(
        lax.psum_scatter(weight_grad(normed, gd), "dp", scatter_dimension=0, tiled=True),
        "seq",
        split_axis=0,
        concat_axis=1,
        tiled=True,
    )
    g_bc = lax.psum_scatter(
        lax.psum(weight_grad(normed_own, gb_own), "head"),
        ("dp", "seq"),
        scatter_dimension=0,
        tiled=True,
    )
    g_out = lax.all_to_all(
        lax.psum_scatter(grad_wo.astype(BF16), "dp", scatter_dimension=1, tiled=True),
        "seq",
        split_axis=1,
        concat_axis=0,
        tiled=True,
    ).astype(F32)

    def whole(x):
        return lax.all_gather(x, "head", axis=0, tiled=True).reshape(micro, seqs, span, model)

    small = lax.psum((d_cxw, d_cxb, d_dtb, d_alog, d_dsk, grad_gain), "dp")
    small = [lax.all_gather(a, "seq", axis=a.ndim - 1, tiled=True) for a in small]
    grad_norm, d_cbw, d_cbb = lax.psum((grad_norm, d_cbw, d_cbb), ("dp", "seq", "head"))
    return (
        whole(result_own),
        whole(grad_own),
        grad_norm,
        g_gate,
        g_x,
        g_bc,
        g_dt,
        small[0],
        small[1],
        d_cbw,
        d_cbb,
        small[2],
        small[3],
        small[4],
        small[5],
        g_out,
    )


def solution(mesh):
    rows = P(("dp", "seq"), "head")
    tok = P(None, "dp", "seq", None)
    return jax.shard_map(
        body,
        mesh=mesh,
        in_specs=(
            tok,
            P(),
            rows,
            rows,
            P(("dp", "seq"), None),
            rows,
            P(None, "head"),
            P("head"),
            P(),
            P(),
            P("head"),
            P("head"),
            P("head"),
            P("head"),
            P("head", ("dp", "seq")),
            P(None, "dp"),
            tok,
        ),
        out_specs=(
            tok,
            tok,
            P(),
            rows,
            rows,
            P(("dp", "seq"), None),
            rows,
            P(None, "head"),
            P("head"),
            P(),
            P(),
            P("head"),
            P("head"),
            P("head"),
            P("head"),
            P("head", ("dp", "seq")),
        ),
        check_vma=False,
    )
```

profile of v0, /device:TPU:14, one launch (start us, length us, event | category | flops | bytes accessed | tf_op | source)
XLA Modules:
  0.0 1105.0 jit_solution(2029383470495228353)
XLA Ops:
  12.0 27.5 %all_to_all.115 = bf16[128,8,256]{0,2,1:T(8,128)(2,1)S(1)} all-to-all(bf16[128,8,256]{0,2,1:T(8,128)(2,1)S(1)} %bitcast.572), channel_id=1, replica_groups=mesh['dp'=2,'seq'=8,'head'=2] {'seq'}, dimensions={1} | all-to-all | bytes 1048576 | tf_op jit(solution)/shard_map/all_to_all | solution.py:139
  41.4 28.8 %all_to_all.116 = bf16[8,256,128]{2,1,0:T(8,128)(2,1)S(1)} all-to-all(bf16[8,256,128]{2,1,0:T(8,128)(2,1)S(1)} %bitcast.582), channel_id=1, replica_groups=mesh['dp'=2,'seq'=8,'head'=2] {'seq'}, dimensions={0} | all-to-all | bytes 1048576 | tf_op jit(solution)/shard_map/all_to_all | solution.py:152
  73.2 8.3 all-to-all-start.1
  83.4 42.2 %all_gather.47 = bf16[2048,32]{0,1:T(8,128)(2,1)S(1)} all-gather(bf16[128,32]{0,1:T(8,128)(2,1)S(1)} %copy-done.97), channel_id=1, replica_groups=mesh['dp'=2,'seq'=8,'head'=2] {'dp','seq'}, dimensions={0}, use_global_device_ids=true | all-gather | bytes 139264 | tf_op jit(solution)/shard_map/all_gather | solution.py:148
  129.6 5.6 fusion.19
  135.8 47.9 %fusion.184 = f32[2,8,128,4]{3,1,2,0:T(8,128)S(1)} fusion(f32[2,8,128,4]{3,1,2,0:T(8,128)S(1)} %copy.524), kind=kOutput, calls=%fused_computation.362 | output fusion | flops 1040384 | bytes 65536 | tf_op jit(solution)/shard_map/jvp(jit(cumsum))/reduce_window_sum | solution.py:41
  184.5 6.0 convolution_convert_fusion.6
  192.2 6.0 convolution_convert_fusion.5
  198.6 12.3 %all-gather.21.cloned.1.call-done = bf16[256,2048]{0,1:T(8,128)(2,1)} async-done(((bf16[256,1024]{0,1:T(8,128)(2,1)}), bf16[256,2048]{0,1:T(8,128)(2,1)}) %all-gather.21.cloned.1.call-update) | async-done | bytes 1048592 | tf_op jit(solution)/shard_map/all_gather | solution.py:151
  210.9 76.9 %all-gather.19.cloned.1.call-done = bf16[2048,2048]{1,0:T(8,128)(2,1)} async-done(((bf16[128,2048]{1,0:T(8,128)(2,1)}), bf16[2048,2048]{1,0:T(8,128)(2,1)}) %all-gather.19.cloned.1.call-update) | async-done | bytes 8388624 | tf_op jit(solution)/shard_map/all_gather | solution.py:157
  287.8 7.3 fusion.188
  295.1 3.0 copy.565
  298.3 11.7 %all-gather.17.cloned.1.call-done = bf16[2048,256]{1,0:T(8,128)(2,1)} async-done(((bf16[1024,256]{1,0:T(8,128)(2,1)}), bf16[2048,256]{1,0:T(8,128)(2,1)}) %all-gather.17.cloned.1.call-update) | async-done | bytes 1048592 | tf_op jit(solution)/shard_map/all_gather | solution.py:138
  310.0 6.0 convolution_convert_fusion.4
  318.4 2.9 copy.560
  321.4 6.9 fusion.44
  328.3 5.1 reshape.593
  333.3 4.9 copy.522
  338.3 2.6 fusion.43
  356.7 10.7 multiply_reduce_fusion.16
  367.4 3.1 copy.559
  370.5 2.6 multiply_reduce_fusion.15
  373.1 48.8 %psum.77 = f32[2,2,1024]{2,1,0:T(2,128)S(1)} all-reduce(f32[2,2,1024]{2,1,0:T(2,128)S(1)} %pad_maximum_fusion), channel_id=1, replica_groups=mesh['dp'=2,'seq'=8,'head'=2] {'seq','head'}, use_global_device_ids=true, to_apply=%region_4.5 | all-reduce | flops 4096 | bytes 32768 | tf_op jit(solution)/shard_map/psum | solution.py:188
  423.2 5.9 multiply_reduce_fusion.13
  429.2 3.6 fusion.72
  436.4 4.5 fusion.69
  440.9 3.3 fusion.111
  447.5 4.5 fusion.78
  452.0 3.2 fusion.51
  455.2 12.5 %fusion.12 = (f32[2,8,128,128]{3,2,1,0:T(8,128)}, f32[2,8,128,128,4]{3,2,4,1,0:T(8,128)}) fusion(f32[2,8,128,4]{2,3,1,0:T(4,128)S(1)} %copy-done.72, pred[2,8,128,128]{3,2,1,0:T(8,128)(4,1)S(1)} %copy-done.51, pred[8,128,128]{2,1,0:T(8,128)(4,1)S(1)} %copy-done.56, f32[2,8,128,128]{3,2,1,0:T(8,128)S(1)} %copy-done.41, ...), kind=kOutput, calls=%fused_computation.18 | convolution fusion | flops 824442880 | bytes 10944512 | tf_op jit(solution)/shard_map/transpose(jvp(sktuh,skuhp->skthp))/dot_general | solution.py:74
  467.7 4.6 fusion.90
  474.5 4.1 fusion.175
  478.7 9.8 multiply_reduce_fusion
  491.9 47.3 %fusion.185 = f32[2,8,128,4]{3,1,2,0:T(8,128)S(1)} fusion(f32[2,8,128,4]{3,1,2,0:T(8,128)S(1)} %copy.609), kind=kOutput, calls=%fused_computation.363 | output fusion | flops 1040384 | bytes 65536 | tf_op jit(solution)/shard_map/transpose(jvp(jit(cumsum)))/reduce_window_sum | solution.py:41
  539.8 4.8 copy.658
  544.6 5.8 reshape.594
  550.5 3.4 multiply_reduce_fusion.10
  566.2 8.1 fusion.156
  574.3 3.2 multiply_reduce_fusion.2
  577.5 8.4 fusion.189
  585.9 16.1 %add_convert_fusion = bf16[2048,2048]{1,0:T(8,128)(2,1)} fusion(f32[2048,2048]{1,0:T(8,128)} %fusion.156, f32[2048,2048]{1,0:T(8,128)} %fusion.189, bf16[2048,256]{1,0:T(8,128)(2,1)S(1)} %bitcast.562, bf16[2048,256]{1,0:T(8,128)(2,1)S(1)} %copy-done.36), kind=kOutput, calls=%fused_computation | convolution fusion | flops 2160066560 | bytes 44040192 | tf_op jit(solution)/shard_map/rc,kc->rk/dot_general | solution.py:212
  603.5 5.6 convolution_convert_fusion
  609.2 6.9 fusion.190
  616.4 6.9 convolution_convert_fusion.3
  623.4 7.0 convolution_convert_fusion.2
  630.4 6.9 convolution_convert_fusion.1
  637.5 2.8 fusion.150
  640.3 105.5 %reduce-scatter.13.cloned.1.call-done = bf16[128,2048]{1,0:T(8,128)(2,1)} async-done(((bf16[2048,2048]{1,0:T(8,128)(2,1)}), bf16[128,2048]{1,0:T(8,128)(2,1)}) %reduce-scatter.13.cloned.1.call-update) | async-done | bytes 524304 | tf_op jit(solution)/shard_map/reduce_scatter | solution.py:218
  747.9 106.9 %reduce-scatter.11.cloned.1.call-done = bf16[128,2048]{1,0:T(8,128)(2,1)} async-done(((bf16[2048,2048]{1,0:T(8,128)(2,1)}), bf16[128,2048]{1,0:T(8,128)(2,1)}) %reduce-scatter.11.cloned.1.call-update) | async-done | bytes 524304 | tf_op jit(solution)/shard_map/reduce_scatter | solution.py:194
  854.8 2.6 fusion.97
  857.4 19.1 %reduce-scatter.25.cloned.1.call-done = f32[1024,4]{1,0:T(8,128)} async-done(((f32[2048,4]{1,0:T(8,128)}), f32[1024,4]{1,0:T(8,128)}) %reduce-scatter.25.cloned.1.call-update) | async-done | bytes 16400
  877.7 10.1 all_to_all.117
  887.8 11.9 %reduce-scatter.17.cloned.1.call-done = bf16[1024,256]{1,0:T(8,128)(2,1)} async-done(((bf16[2048,256]{1,0:T(8,128)(2,1)}), bf16[1024,256]{1,0:T(8,128)(2,1)}) %reduce-scatter.17.cloned.1.call-update) | async-done | bytes 524304 | tf_op jit(solution)/shard_map/reduce_scatter | solution.py:227
  899.7 6.0 all-to-all-start.3
  906.3 16.5 %reduce-scatter.19.cloned.1.call-done = bf16[1024,256]{1,0:T(8,128)(2,1)} async-done(((bf16[2048,256]{1,0:T(8,128)(2,1)}), bf16[1024,256]{1,0:T(8,128)(2,1)}) %reduce-scatter.19.cloned.1.call-update) | async-done | bytes 524304 | tf_op jit(solution)/shard_map/reduce_scatter | solution.py:227
  922.8 6.0 all-to-all-start.4
  930.3 15.1 %reduce-scatter.21.cloned.1.call-done = bf16[256,1024]{1,0:T(8,128)(2,1)} async-done(((bf16[256,2048]{1,0:T(8,128)(2,1)}), bf16[256,1024]{1,0:T(8,128)(2,1)}) %reduce-scatter.21.cloned.1.call-update) | async-done | bytes 524304 | tf_op jit(solution)/shard_map/reduce_scatter | solution.py:249
  947.3 6.0 all-to-all-start.6
  953.5 5.0 all-reduce.54
  958.5 19.4 %all-gather = f32[8,1,256]{2,1,0:T(1,128)S(1)} all-gather(f32[1,1,256]{2,1,0:T(1,128)S(1)} %bitcast.633), channel_id=1, replica_groups=mesh['dp'=2,'seq'=8,'head'=2] {'seq'}, dimensions={0}, use_global_device_ids=true | all-gather | bytes 9216 | tf_op jit(solution)/shard_map/all_gather | solution.py:260
  977.9 15.5 %all-gather.1 = f32[8,1,256]{2,1,0:T(1,128)S(1)} all-gather(f32[1,1,256]{2,1,0:T(1,128)S(1)} %bitcast.632), channel_id=1, replica_groups=mesh['dp'=2,'seq'=8,'head'=2] {'seq'}, dimensions={0}, use_global_device_ids=true | all-gather | bytes 9216 | tf_op jit(solution)/shard_map/all_gather | solution.py:260
  993.4 27.9 %all_gather.54 = f32[4,2048]{1,0:T(4,128)S(1)} all-gather(f32[4,256]{1,0:T(4,128)S(1)} %get-tuple-element.164), channel_id=1, replica_groups=mesh['dp'=2,'seq'=8,'head'=2] {'seq'}, dimensions={1}, use_global_device_ids=true | all-gather | bytes 36864 | tf_op jit(solution)/shard_map/all_gather | solution.py:260
  1021.9 22.0 %all-reduce.53 = (f32[32]{0:T(128)}, f32[32]{0:T(128)}, f32[32]{0:T(128)}) all-reduce(f32[32]{0:T(128)S(1)} %dynamic-update-slice, f32[32]{0:T(128)S(1)} %dynamic-update-slice.1, f32[32]{0:T(128)S(1)} %dynamic-update-slice.2), channel_id=1, replica_groups=mesh['dp'=2,'seq'=8,'head'=2] {'seq'}, use_global_device_ids=true, to_apply=%add.49 | all-reduce | flops 96 | bytes 768
  1047.4 43.9 %all-reduce.52 = (f32[2048]{0:T(1024)}, f32[4,256]{1,0:T(4,128)}, f32[256]{0:T(256)}) all-reduce(f32[2048]{0:T(1024)S(1)} %get-tuple-element.135, f32[4,256]{1,0:T(4,128)S(1)} %pad_add_fusion.10, f32[256]{0:T(256)S(1)} %get-tuple-element.131), channel_id=1, replica_groups=mesh['dp'=2,'seq'=8,'head'=2] {'dp','seq','head'}, use_global_device_ids=true, to_apply=%region_33.34 | all-reduce | flops 3328 | bytes 26624 | tf_op jit(solution)/shard_map/psum | solution.py:261
  (405 shorter events, 82.8 us)
Async XLA Ops:
  7.2 122.4 %all-gather.11.cloned.1.call-start = ((), (), s32[]{:S(2)}) async-start(), calls=%async_computation.15 | async-start | bytes 8912896 | tf_op jit(solution)/shard_map/all_gather | solution.py:135
  11.7 29.7 %copy-start.47 = (bf16[2048,128]{1,0:T(8,128)(2,1)S(1)}, bf16[2048,128]{1,0:T(8,128)(2,1)}, u32[]{:S(2)}) copy-start(bf16[2048,128]{1,0:T(8,128)(2,1)} %param.31) | copy-start | bytes 1572868
  11.7 172.8 %all-gather.13.cloned.1.call-start = ((), (), s32[]{:S(2)}) async-start(), calls=%async_computation.16 | async-start | bytes 1572864 | tf_op jit(solution)/shard_map/all_gather | solution.py:138
  39.5 31.8 %copy-start.43 = (bf16[2,1,128,2048]{3,2,1,0:T(8,128)(2,1)S(1)}, bf16[2,1,128,2048]{3,2,1,0:T(8,128)(2,1)}, u32[]{:S(2)}) copy-start(bf16[2,1,128,2048]{3,2,1,0:T(8,128)(2,1)} %param.33) | copy-start | bytes 3145732
  40.6 151.7 %all-gather.15.cloned.1.call-start = ((), (), s32[]{:S(2)}) async-start(), calls=%async_computation.17 | async-start | bytes 1114112 | tf_op jit(solution)/shard_map/all_gather | solution.py:150
  41.3 169.6 %all-gather.21.cloned.1.call-start = ((), (), s32[]{:S(2)}) async-start(), calls=%async_computation.20 | async-start | bytes 1572864 | tf_op jit(solution)/shard_map/all_gather | solution.py:151
  41.4 30.9 %copy-start.48 = (bf16[128,2048]{1,0:T(8,128)(2,1)S(1)}, bf16[128,2048]{1,0:T(8,128)(2,1)}, u32[]{:S(2)}) copy-start(bf16[128,2048]{1,0:T(8,128)(2,1)} %param.19) | copy-start | bytes 1572868
  71.2 12.1 %copy-start.97 = (bf16[128,32]{0,1:T(8,128)(2,1)S(1)}, bf16[128,32]{0,1:T(8,128)(2,1)}, u32[]{:S(2)}) copy-start(bf16[128,32]{0,1:T(8,128)(2,1)} %param.22) | copy-start | bytes 24580
  71.3 54.3 %copy-start.112 = (f32[32]{0:T(128)S(1)}, f32[32]{0:T(128)}, u32[]{:S(2)}) copy-start(f32[32]{0:T(128)} %param.27) | copy-start | bytes 388
  71.3 54.4 %copy-start.113 = (f32[32]{0:T(128)S(1)}, f32[32]{0:T(128)}, u32[]{:S(2)}) copy-start(f32[32]{0:T(128)} %param.29) | copy-start | bytes 388
  71.3 56.6 %copy-start.108 = (s32[2,1]{0,1:T(1,128)S(1)}, s32[2,1]{0,1:T(1,128)}, u32[]{:S(2)}) copy-start(s32[2,1]{0,1:T(1,128)} %param.32) | copy-start | bytes 28
  71.3 56.7 %copy-start.104 = (f32[4,256]{1,0:T(4,128)S(1)}, f32[4,256]{1,0:T(4,128)}, u32[]{:S(2)}) copy-start(f32[4,256]{1,0:T(4,128)} %param.25) | copy-start | bytes 12292
  71.3 216.5 %all-gather.19.cloned.1.call-start = ((), (), s32[]{:S(2)}) async-start(), calls=%async_computation.19 | async-start | bytes 8912896 | tf_op jit(solution)/shard_map/all_gather | solution.py:157
  73.2 55.2 %all-to-all-start.1 = ((bf16[128,8,256]{0,2,1:T(8,128)(2,1)}), bf16[128,8,256]{0,2,1:T(8,128)(2,1)S(1)}, u32[]{:S(2)}, u32[]{:S(2)}) async-start(bf16[128,8,256]{0,2,1:T(8,128)(2,1)} %bitcast.42), calls=%async_computation.1 | async-start | bytes 1048576 | tf_op jit(solution)/shard_map/all_to_all | solution.py:139
  81.6 228.4 %all-gather.17.cloned.1.call-start = ((), (), s32[]{:S(2)}) async-start(), calls=%async_computation.18 | async-start | bytes 1572864 | tf_op jit(solution)/shard_map/all_gather | solution.py:138
  81.7 53.6 %copy-start.100 = (f32[4]{0:T(128)}, f32[4]{0:T(128)S(1)}, u32[]{:S(2)}) copy-start(f32[4]{0:T(128)S(1)} %fusion.174) | copy-start | bytes 52
  82.6 238.7 %copy-start.81 = (f32[1,256]{1,0:T(1,128)}, f32[1,256]{1,0:T(1,128)S(1)}, u32[]{:S(2)}) copy-start(f32[1,256]{1,0:T(1,128)S(1)} %get-tuple-element.230) | copy-start | bytes 3076
  82.6 238.7 %copy-start.83 = (f32[1,256]{1,0:T(1,128)}, f32[1,256]{1,0:T(1,128)S(1)}, u32[]{:S(2)}) copy-start(f32[1,256]{1,0:T(1,128)S(1)} %get-tuple-element.231) | copy-start | bytes 3076
  82.6 238.7 %copy-start.85 = (f32[1,256]{1,0:T(1,128)}, f32[1,256]{1,0:T(1,128)S(1)}, u32[]{:S(2)}) copy-start(f32[1,256]{1,0:T(1,128)S(1)} %get-tuple-element.232) | copy-start | bytes 3076
  82.6 238.7 %copy-start.87 = (f32[1,256]{1,0:T(1,128)}, f32[1,256]{1,0:T(1,128)S(1)}, u32[]{:S(2)}) copy-start(f32[1,256]{1,0:T(1,128)S(1)} %get-tuple-element.233) | copy-start | bytes 3076
  125.7 230.9 %copy-start.115 = (f32[4]{0:T(128)}, f32[4]{0:T(128)S(1)}, u32[]{:S(2)}) copy-start(f32[4]{0:T(128)S(1)} %dynamic_slice.33) | copy-start | bytes 52
  128.0 70.2 %copy-start.67 = (pred[2,8,128]{2,1,0:T(8,128)(4,1)}, pred[2,8,128]{2,1,0:T(8,128)(4,1)S(1)}, u32[]{:S(2)}) copy-start(pred[2,8,128]{2,1,0:T(8,128)(4,1)S(1)} %broadcast_compare_fusion.2) | copy-start | bytes 6148
  128.0 210.3 %copy-start.89 = (f32[1,256]{1,0:T(1,128)}, f32[1,256]{1,0:T(1,128)S(1)}, u32[]{:S(2)}) copy-start(f32[1,256]{1,0:T(1,128)S(1)} %get-tuple-element.239) | copy-start | bytes 3076
  128.0 210.3 %copy-start.91 = (f32[1,256]{1,0:T(1,128)}, f32[1,256]{1,0:T(1,128)S(1)}, u32[]{:S(2)}) copy-start(f32[1,256]{1,0:T(1,128)S(1)} %get-tuple-element.240) | copy-start | bytes 3076
  128.0 210.3 %copy-start.93 = (f32[1,256]{1,0:T(1,128)}, f32[1,256]{1,0:T(1,128)S(1)}, u32[]{:S(2)}) copy-start(f32[1,256]{1,0:T(1,128)S(1)} %get-tuple-element.241) | copy-start | bytes 3076
  128.0 210.3 %copy-start.95 = (f32[1,256]{1,0:T(1,128)}, f32[1,256]{1,0:T(1,128)S(1)}, u32[]{:S(2)}) copy-start(f32[1,256]{1,0:T(1,128)S(1)} %get-tuple-element.242) | copy-start | bytes 3076
  128.3 228.4 %copy-start.55 = (pred[8,128,128]{2,1,0:T(8,128)(4,1)}, pred[8,128,128]{2,1,0:T(8,128)(4,1)S(1)}, u32[]{:S(2)}) copy-start(pred[8,128,128]{2,1,0:T(8,128)(4,1)S(1)} %get-tuple-element.237) | copy-start | bytes 393220
  128.4 228.2 %copy-start.50 = (pred[2,8,128,128]{3,2,1,0:T(8,128)(4,1)}, pred[2,8,128,128]{3,2,1,0:T(8,128)(4,1)S(1)}, u32[]{:S(2)}) copy-start(pred[2,8,128,128]{3,2,1,0:T(8,128)(4,1)S(1)} %broadcast_and_fusion) | copy-start | bytes 786436
  129.5 508.0 %reduce-scatter.15.cloned.1.call-start = ((), (), s32[]{:S(2)}) async-start(), calls=%async_computation.24 | async-start | bytes 2228224 | tf_op jit(solution)/shard_map/reduce_scatter | solution.py:207
  184.5 172.2 %copy-start.71 = (f32[2,8,128,4]{2,3,1,0:T(4,128)}, f32[2,8,128,4]{2,3,1,0:T(4,128)S(1)}, u32[]{:S(2)}) copy-start(f32[2,8,128,4]{2,3,1,0:T(4,128)S(1)} %copy.525) | copy-start | bytes 98308
  198.4 148.2 %copy-start.59 = (f32[2,8,128,4]{2,3,1,0:T(4,128)}, f32[2,8,128,4]{2,3,1,0:T(4,128)S(1)}, u32[]{:S(2)}) copy-start(f32[2,8,128,4]{2,3,1,0:T(4,128)S(1)} %copy.546) | copy-start | bytes 98308
  198.6 139.7 %copy-start = (f32[8,2,128,256]{3,2,0,1:T(8,128)}, f32[8,2,128,256]{3,2,0,1:T(8,128)S(1)}, u32[]{:S(2)}) copy-start(f32[8,2,128,256]{3,2,0,1:T(8,128)S(1)} %copy.523) | copy-start | bytes 6291460
  298.3 47.0 %copy-start.76 = (f32[2,4]{1,0:T(2,128)}, f32[2,4]{1,0:T(2,128)S(1)}, u32[]{:S(2)}) copy-start(f32[2,4]{1,0:T(2,128)S(1)} %get-tuple-element.150) | copy-start | bytes 100
  298.3 50.6 %copy-start.63 = (f32[2,4]{1,0:T(2,128)}, f32[2,4]{1,0:T(2,128)S(1)}, u32[]{:S(2)}) copy-start(f32[2,4]{1,0:T(2,128)S(1)} %get-tuple-element.154) | copy-start | bytes 100
  298.3 50.6 %copy-start.65 = (f32[2,4]{1,0:T(2,128)}, f32[2,4]{1,0:T(2,128)S(1)}, u32[]{:S(2)}) copy-start(f32[2,4]{1,0:T(2,128)S(1)} %get-tuple-element.157) | copy-start | bytes 100
  298.3 51.1 %copy-start.74 = (f32[2,4]{1,0:T(2,128)}, f32[2,4]{1,0:T(2,128)S(1)}, u32[]{:S(2)}) copy-start(f32[2,4]{1,0:T(2,128)S(1)} %get-tuple-element.151) | copy-start | bytes 100
  341.1 13.2 %copy-start.3 = (f32[2,1024,128]{2,1,0:T(8,128)}, f32[2,1024,128]{2,1,0:T(8,128)S(1)}, u32[]{:S(2)}) copy-start(f32[2,1024,128]{2,1,0:T(8,128)S(1)} %get-tuple-element.221) | copy-start | bytes 3145732
  354.2 13.1 %copy-start.27 = (f32[2,8,128,4,64]{2,4,3,1,0:T(8,128)}, f32[2,8,128,4,64]{2,4,3,1,0:T(8,128)S(1)}, u32[]{:S(2)}) copy-start(f32[2,8,128,4,64]{2,4,3,1,0:T(8,128)S(1)} %fusion.55) | copy-start | bytes 6291460
  455.2 12.5 %copy-start.20 = (f32[2,8,4,64,128]{4,3,2,0,1:T(8,128)S(1)}, f32[2,8,4,64,128]{4,3,2,0,1:T(8,128)}, u32[]{:S(2)}) copy-start(f32[2,8,4,64,128]{4,3,2,0,1:T(8,128)} %copy-done.19) | copy-start | bytes 6291460
  491.5 48.1 %copy-start.53 = (f32[2,8,128,4]{2,3,1,0:T(4,128)S(1)}, f32[2,8,128,4]{2,3,1,0:T(4,128)}, u32[]{:S(2)}) copy-start(f32[2,8,128,4]{2,3,1,0:T(4,128)} %get-tuple-element.137) | copy-start | bytes 98308
  491.5 48.1 %copy-start.101 = (f32[4]{0:T(128)S(1)}, f32[4]{0:T(128)}, u32[]{:S(2)}) copy-start(f32[4]{0:T(128)} %copy-done.100) | copy-start | bytes 52
  491.5 48.1 %copy-start.103 = (f32[4]{0:T(128)S(1)}, f32[4]{0:T(128)}, u32[]{:S(2)}) copy-start(f32[4]{0:T(128)} %copy-done.102) | copy-start | bytes 52
  566.1 179.7 %reduce-scatter.13.cloned.1.call-start = ((), (), s32[]{:S(2)}) async-start(), calls=%async_computation.23 | async-start | bytes 8912896 | tf_op jit(solution)/shard_map/reduce_scatter | solution.py:218
  602.0 252.8 %reduce-scatter.11.cloned.1.call-start = ((), (), s32[]{:S(2)}) async-start(), calls=%async_computation.21 | async-start | bytes 8912896 | tf_op jit(solution)/shard_map/reduce_scatter | solution.py:194
  609.1 267.4 %reduce-scatter.25.cloned.1.call-start = ((), (), s32[]{:S(2)}) async-start(), calls=%async_computation.31 | async-start | bytes 1572864
  616.1 283.6 %reduce-scatter.17.cloned.1.call-start = ((), (), s32[]{:S(2)}) async-start(), calls=%async_computation.26 | async-start | bytes 1572864 | tf_op jit(solution)/shard_map/reduce_scatter | solution.py:227
  623.3 299.5 %reduce-scatter.19.cloned.1.call-start = ((), (), s32[]{:S(2)}) async-start(), calls=%async_computation.27 | async-start | bytes 1572864 | tf_op jit(solution)/shard_map/reduce_scatter | solution.py:227
  630.4 315.0 %reduce-scatter.21.cloned.1.call-start = ((), (), s32[]{:S(2)}) async-start(), calls=%async_computation.28 | async-start | bytes 1572864 | tf_op jit(solution)/shard_map/reduce_scatter | solution.py:249
  637.3 108.5 %copy-start.31 = (bf16[2,1,128,2048]{3,2,1,0:T(8,128)(2,1)S(1)}, bf16[2,1,128,2048]{3,2,1,0:T(8,128)(2,1)}, u32[]{:S(2)}) copy-start(bf16[2,1,128,2048]{3,2,1,0:T(8,128)(2,1)} %param.17) | copy-start | bytes 3145732
  637.3 108.5 %copy-start.62 = (f32[2048]{0:T(1024)S(1)}, f32[2048]{0:T(1024)}, u32[]{:S(2)}) copy-start(f32[2048]{0:T(1024)} %param.18) | copy-start | bytes 24580
  637.4 108.5 %copy-start.99 = (f32[128]{0:T(128)S(1)}, f32[128]{0:T(128)}, u32[]{:S(2)}) copy-start(f32[128]{0:T(128)} %copy-done.98) | copy-start | bytes 1540
  637.4 406.7 %reduce-scatter.23.cloned.1.call-start = ((), (), s32[]{:S(2)}) async-start(), calls=%async_computation.29 | async-start | bytes 2228224 | tf_op jit(solution)/shard_map/reduce_scatter | solution.py:242
  637.5 108.4 %copy-start.49 = (f32[128,256]{1,0:T(8,128)S(1)}, f32[128,256]{1,0:T(8,128)}, u32[]{:S(2)}) copy-start(f32[128,256]{1,0:T(8,128)} %reduce-scatter.15.cloned.1.call-done) | copy-start | bytes 393220
  640.3 107.6 %copy-start.111 = (f32[128]{0:T(128)S(1)}, f32[128]{0:T(128)}, u32[]{:S(2)}) copy-start(f32[128]{0:T(128)} %copy-done.110) | copy-start | bytes 1540
  640.3 214.5 %copy-start.44 = (bf16[2,1,128,2048]{3,2,1,0:T(8,128)(2,1)S(1)}, bf16[2,1,128,2048]{3,2,1,0:T(8,128)(2,1)}, u32[]{:S(2)}) copy-start(bf16[2,1,128,2048]{3,2,1,0:T(8,128)(2,1)} %param.33) | copy-start | bytes 3145732
  640.3 451.1 %all-gather.23.cloned.1.call-start = ((), (), s32[]{:S(2)}) async-start(), calls=%async_computation.22 | async-start | bytes 1572864 | tf_op jit(solution)/shard_map/all_gather | solution.py:257
  857.4 71.5 %copy-start.114 = (u32[32]{0:T(128)S(1)}, u32[32]{0:T(128)}, u32[]{:S(2)}) copy-start(u32[32]{0:T(128)} %constant.176) | copy-start | bytes 388
  899.7 23.1 %all-to-all-start.3 = ((bf16[8,128,256]{2,1,0:T(8,128)(2,1)}), bf16[8,128,256]{2,1,0:T(8,128)(2,1)S(1)}, u32[]{:S(2)}, u32[]{:S(2)}) async-start(bf16[8,128,256]{2,1,0:T(8,128)(2,1)} %bitcast.584), calls=%async_computation.7 | async-start | bytes 1048576 | tf_op jit(solution)/shard_map/all_to_all | solution.py:226
  905.7 185.6 %all-gather.25.cloned.1.call-start = ((), (), s32[]{:S(2)}) async-start(), calls=%async_computation.25 | async-start | bytes 3145728 | tf_op jit(solution)/shard_map/all_gather | solution.py:257
  905.7 47.7 %copy-start.107 = (f32[32]{0:T(128)S(1)}, f32[32]{0:T(128)}, u32[]{:S(2)}) copy-start(f32[32]{0:T(128)} %param.28) | copy-start | bytes 388
  905.7 47.7 %copy-start.109 = (f32[4]{0:T(128)S(1)}, f32[4]{0:T(128)}, u32[]{:S(2)}) copy-start(f32[4]{0:T(128)} %get-tuple-element.130) | copy-start | bytes 52
  922.8 24.5 %all-to-all-start.4 = ((bf16[8,128,256]{2,1,0:T(8,128)(2,1)}), bf16[8,128,256]{2,1,0:T(8,128)(2,1)S(1)}, u32[]{:S(2)}, u32[]{:S(2)}) async-start(bf16[8,128,256]{2,1,0:T(8,128)(2,1)} %bitcast.583), calls=%async_computation.9 | async-start | bytes 1048576 | tf_op jit(solution)/shard_map/all_to_all | solution.py:226
  947.3 99.0 %all-to-all-start.6 = ((bf16[256,8,128]{2,0,1:T(8,128)(2,1)}), bf16[256,8,128]{2,0,1:T(8,128)(2,1)S(1)}, u32[]{:S(2)}, u32[]{:S(2)}) async-start(bf16[256,8,128]{2,0,1:T(8,128)(2,1)} %copy_bitcast_fusion), calls=%async_computation.12 | async-start | bytes 1048576 | tf_op jit(solution)/shard_map/all_to_all | solution.py:248
  953.4 138.0 %all-reduce.57.cloned.1.call-start = ((), (), s32[]{:S(2)}) async-start(), calls=%async_computation.30 | async-start | bytes 262144 | tf_op jit(solution)/shard_map/psum | solution.py:243
  (74 other events, 294.3 us)
Sparse Core Ops, SparseCore 0:
  11.8 92.2 all-gather.10
  106.2 24.0 all-gather.12
  133.1 54.8 all-gather.14
  190.0 20.8 all-gather.20
  213.5 74.2 all-gather.18
  289.8 20.1 all-gather.16
  566.2 70.9 reduce-scatter.14
  641.8 103.9 reduce-scatter.12
  750.4 104.3 reduce-scatter.10
  857.6 18.9 reduce-scatter.24
  879.3 20.3 reduce-scatter.16
  902.5 20.3 reduce-scatter.18
  925.1 20.3 reduce-scatter.20
  948.2 76.7 reduce-scatter.22
  1026.4 14.1 all-gather.22
  1042.7 11.7 all-gather.24
  1056.8 19.0 all-reduce.56
where the time goes:
time: 1110 us; the launch traced here: 1100 us
  waiting for transfers between devices  377 us (34%)
  blocking collectives  291 us (26%)
  matrix products  176 us (16%)
  other arithmetic  145 us (13%)
  local copies, waits for them, and re-layouts  72 us (6%)
  starting transfers between devices  27.2 us (2%)
  between operations  16.4 us (1%)
    reduce_scatter x1, waiting for transfers between devices, body(): lax.psum_scatter(dot_f32(scaled, wo).astype(BF16), everyone, scatter_dime...  107 us
    reduce_scatter x1, waiting for transfers between devices, body(): lax.psum_scatter(part_normed.astype(BF16), everyone, scatter_dimension=0,...  105 us
    another operation x2, other arithmetic, mixer(): cum = jnp.cumsum(dt * -jnp.exp(a_log), axis=2)  95.2 us
    all_gather x1, waiting for transfers between devices, body(): cot = lax.all_gather(my_cot, everyone, axis=0, tiled=True)  76.9 us
    all_gather x3, blocking collectives, body(): lax.all_gather(a, 'seq', axis=a.ndim - 1, tiled=True)  62.8 us
    psum x1, blocking collectives, body(): lax.psum(jnp.stack([jnp.sum(gated * gated, axis=-1), jnp.sum(gs * gated,...  48.8 us
    psum x1, blocking collectives, body(): lax.psum((grad_norm, d_cbw, d_cbb), ('dp', 'seq', 'head'))  43.9 us
    all_gather x1, blocking collectives, body(): lax.all_gather(w_dt_in, ('dp', 'seq'), axis=0, tiled=True)  42.2 us
  transfers between devices with their start and end apart: 21, of which 9 were waited for; matrix products, arithmetic and copies ran while one was open for 16% of the time, Pallas kernels for 0%

commit v1 on v0

--- a/solution.py
+++ b/solution.py
@@ -1,3 +1,4 @@
+import functools
 import jax
 import jax.numpy as jnp
 from jax import lax
@@ -8,6 +9,21 @@
 BF16 = jnp.bfloat16
 F32 = jnp.float32
 CHUNK = 128
+
+
+def work_the_table(t0, dim_no, array_axis):
+    return jnp.concatenate(
+        lax.all_to_all(
+            jnp.stack(jnp.split(t0, lax.psum(1, axis_name="seq"), dim_no)),
+            axis_name="seq",
+            split_axis=0,
+            concat_axis=0,
+        ),
+        array_axis,
+    )
+
+
+list_loads_now = functools.partial(work_the_table, dim_no=0, array_axis=1)
 
 
 def dot_f32(a, b):
@@ -148,12 +164,7 @@
         lax.all_gather(w_dt_in, ("dp", "seq"), axis=0, tiled=True), me_seq * heads, heads, 1
     )
     wb = lax.all_gather(w_bc_in, ("dp", "seq"), axis=0, tiled=True)
-    wo = lax.all_gather(
-        lax.all_to_all(w_out, "seq", split_axis=0, concat_axis=1, tiled=True),
-        "dp",
-        axis=1,
-        tiled=True,
-    )
+    wo = lax.all_gather(list_loads_now(w_out), "dp", axis=1, tiled=True)
     cot = lax.all_gather(my_cot, everyone, axis=0, tiled=True)
 
     def part(x, size, axis):

time: 1110 us -> 1110 us (level)
    unnamed x258 -> x273, local copies, waits for them, and re-layouts: 22.8 us -> 23.6 us
where the time goes in v1:
time: 1110 us
  waiting for transfers between devices  376 us (34%)
  blocking collectives  294 us (26%)
  matrix products  176 us (16%)
  other arithmetic  145 us (13%)
  local copies, waits for them, and re-layouts  71.9 us (6%)
  starting transfers between devices  26.4 us (2%)
  between operations  16.6 us (1%)
    reduce_scatter x1, waiting for transfers between devices, body(): lax.psum_scatter(dot_f32(scaled, wo).astype(BF16), everyone, scatter_dime...  107 us
    reduce_scatter x1, waiting for transfers between devices, body(): lax.psum_scatter(part_normed.astype(BF16), everyone, scatter_dimension=0,...  105 us
    another operation x2, other arithmetic, mixer(): cum = jnp.cumsum(dt * -jnp.exp(a_log), axis=2)  95.2 us
    all_gather x1, waiting for transfers between devices, body(): cot = lax.all_gather(my_cot, everyone, axis=0, tiled=True)  76.9 us
    all_gather x3, blocking collectives, body(): lax.all_gather(a, 'seq', axis=a.ndim - 1, tiled=True)  62.7 us
    psum x1, blocking collectives, body(): lax.psum(jnp.stack([jnp.sum(gated * gated, axis=-1), jnp.sum(gs * gated,...  48.8 us
    psum x1, blocking collectives, body(): lax.psum((grad_norm, d_cbw, d_cbb), ('dp', 'seq', 'head'))  43.8 us
    all_gather x1, blocking collectives, body(): lax.all_gather(w_dt_in, ('dp', 'seq'), axis=0, tiled=True)  42.9 us
  transfers between devices with their start and end apart: 21, of which 9 were waited for; matrix products, arithmetic and copies ran while one was open for 16% of the time, Pallas kernels for 0%

profile of v1, /device:TPU:14, one launch (start us, length us, event | category | flops | bytes accessed | tf_op | source)
XLA Modules:
  0.0 1105.5 jit_solution(6930239819836706075)
XLA Ops:
  12.0 27.5 %all_to_all.101 = bf16[128,8,256]{0,2,1:T(8,128)(2,1)S(1)} all-to-all(bf16[128,8,256]{0,2,1:T(8,128)(2,1)S(1)} %bitcast.588), channel_id=1, replica_groups=mesh['dp'=2,'seq'=8,'head'=2] {'seq'}, dimensions={1} | all-to-all | bytes 1048576 | tf_op jit(solution)/shard_map/all_to_all | solution.py:155
  42.5 30.4 %all_to_all.102 = bf16[8,256,128]{1,2,0:T(8,128)(2,1)} all-to-all(bf16[8,256,128]{1,2,0:T(8,128)(2,1)S(1)} %bitcast_dynamic-update-slice_fusion.6), channel_id=1, replica_groups=mesh['dp'=2,'seq'=8,'head'=2] {'seq'}, dimensions={0} | all-to-all | bytes 1048576 | tf_op jit(solution)/shard_map/all_to_all | solution.py:16
  74.9 7.4 all-to-all-start.1
  84.1 42.9 %all_gather.47 = bf16[2048,32]{0,1:T(8,128)(2,1)S(1)} all-gather(bf16[128,32]{0,1:T(8,128)(2,1)S(1)} %copy-done.97), channel_id=1, replica_groups=mesh['dp'=2,'seq'=8,'head'=2] {'dp','seq'}, dimensions={0}, use_global_device_ids=true | all-gather | bytes 139264 | tf_op jit(solution)/shard_map/all_gather | solution.py:164
  131.0 5.6 fusion.19
  137.2 47.9 %fusion.185 = f32[2,8,128,4]{3,1,2,0:T(8,128)S(1)} fusion(f32[2,8,128,4]{3,1,2,0:T(8,128)S(1)} %copy.553), kind=kOutput, calls=%fused_computation.371 | output fusion | flops 1040384 | bytes 65536 | tf_op jit(solution)/shard_map/jvp(jit(cumsum))/reduce_window_sum | solution.py:57
  185.9 6.0 convolution_convert_fusion.6
  193.7 6.0 convolution_convert_fusion.5
  200.1 11.3 %all-gather.21.cloned.1.call-done = bf16[256,2048]{0,1:T(8,128)(2,1)} async-done(((bf16[256,1024]{0,1:T(8,128)(2,1)}), bf16[256,2048]{0,1:T(8,128)(2,1)}) %all-gather.21.cloned.1.call-update) | async-done | bytes 1048592 | tf_op jit(solution)/shard_map/all_gather | solution.py:167
  211.4 76.9 %all-gather.19.cloned.1.call-done = bf16[2048,2048]{1,0:T(8,128)(2,1)} async-done(((bf16[128,2048]{1,0:T(8,128)(2,1)}), bf16[2048,2048]{1,0:T(8,128)(2,1)}) %all-gather.19.cloned.1.call-update) | async-done | bytes 8388624 | tf_op jit(solution)/shard_map/all_gather | solution.py:168
  288.3 7.3 fusion.189
  295.6 3.0 copy.601
  298.8 11.7 %all-gather.17.cloned.1.call-done = bf16[2048,256]{1,0:T(8,128)(2,1)} async-done(((bf16[1024,256]{1,0:T(8,128)(2,1)}), bf16[2048,256]{1,0:T(8,128)(2,1)}) %all-gather.17.cloned.1.call-update) | async-done | bytes 1048592 | tf_op jit(solution)/shard_map/all_gather | solution.py:154
  310.5 6.0 convolution_convert_fusion.4
  318.9 2.9 copy.589
  321.9 6.9 fusion.44
  328.7 5.1 reshape.598
  333.8 4.9 copy.551
  338.8 2.6 fusion.43
  357.1 10.7 multiply_reduce_fusion.16
  367.9 3.1 copy.588
  370.9 2.6 multiply_reduce_fusion.15
  373.6 48.8 %psum.77 = f32[2,2,1024]{2,1,0:T(2,128)S(1)} all-reduce(f32[2,2,1024]{2,1,0:T(2,128)S(1)} %pad_maximum_fusion), channel_id=1, replica_groups=mesh['dp'=2,'seq'=8,'head'=2] {'seq','head'}, use_global_device_ids=true, to_apply=%region_4.5 | all-reduce | flops 4096 | bytes 32768 | tf_op jit(solution)/shard_map/psum | solution.py:199
  423.7 5.9 multiply_reduce_fusion.13
  429.6 3.6 fusion.72
  436.9 4.5 fusion.69
  441.3 3.3 fusion.111
  447.9 4.5 fusion.78
  452.5 3.2 fusion.51
  455.7 12.5 %fusion.12 = (f32[2,8,128,128]{3,2,1,0:T(8,128)}, f32[2,8,128,128,4]{3,2,4,1,0:T(8,128)}) fusion(f32[2,8,128,4]{2,3,1,0:T(4,128)S(1)} %copy-done.72, pred[2,8,128,128]{3,2,1,0:T(8,128)(4,1)S(1)} %copy-done.51, pred[8,128,128]{2,1,0:T(8,128)(4,1)S(1)} %copy-done.56, f32[2,8,128,128]{3,2,1,0:T(8,128)S(1)} %copy-done.41, ...), kind=kOutput, calls=%fused_computation.18 | convolution fusion | flops 824442880 | bytes 10944512 | tf_op jit(solution)/shard_map/transpose(jvp(sktuh,skuhp->skthp))/dot_general | solution.py:90
  468.2 4.6 fusion.90
  475.0 4.1 fusion.175
  479.2 9.8 multiply_reduce_fusion
  492.4 47.3 %fusion.186 = f32[2,8,128,4]{3,1,2,0:T(8,128)S(1)} fusion(f32[2,8,128,4]{3,1,2,0:T(8,128)S(1)} %copy.645), kind=kOutput, calls=%fused_computation.372 | output fusion | flops 1040384 | bytes 65536 | tf_op jit(solution)/shard_map/transpose(jvp(jit(cumsum)))/reduce_window_sum | solution.py:57
  540.3 4.8 copy.694
  545.0 5.9 reshape.599
  550.9 3.4 multiply_reduce_fusion.10
  566.6 8.1 fusion.156
  574.8 3.2 multiply_reduce_fusion.2
  578.0 8.4 fusion.190
  586.4 16.1 %add_convert_fusion = bf16[2048,2048]{1,0:T(8,128)(2,1)} fusion(f32[2048,2048]{1,0:T(8,128)} %fusion.156, f32[2048,2048]{1,0:T(8,128)} %fusion.190, bf16[2048,256]{1,0:T(8,128)(2,1)S(1)} %bitcast.578, bf16[2048,256]{1,0:T(8,128)(2,1)S(1)} %copy-done.36), kind=kOutput, calls=%fused_computation | convolution fusion | flops 2160066560 | bytes 44040192 | tf_op jit(solution)/shard_map/rc,kc->rk/dot_general | solution.py:223
  604.0 5.6 convolution_convert_fusion
  609.7 6.9 fusion.191
  616.9 6.9 convolution_convert_fusion.3
  623.9 7.0 convolution_convert_fusion.2
  630.9 6.9 convolution_convert_fusion.1
  638.0 2.8 fusion.150
  640.8 105.4 %reduce-scatter.13.cloned.1.call-done = bf16[128,2048]{1,0:T(8,128)(2,1)} async-done(((bf16[2048,2048]{1,0:T(8,128)(2,1)}), bf16[128,2048]{1,0:T(8,128)(2,1)}) %reduce-scatter.13.cloned.1.call-update) | async-done | bytes 524304 | tf_op jit(solution)/shard_map/reduce_scatter | solution.py:229
  748.3 107.0 %reduce-scatter.11.cloned.1.call-done = bf16[128,2048]{1,0:T(8,128)(2,1)} async-done(((bf16[2048,2048]{1,0:T(8,128)(2,1)}), bf16[128,2048]{1,0:T(8,128)(2,1)}) %reduce-scatter.11.cloned.1.call-update) | async-done | bytes 524304 | tf_op jit(solution)/shard_map/reduce_scatter | solution.py:205
  855.3 2.6 fusion.97
  857.9 19.1 %reduce-scatter.25.cloned.1.call-done = f32[1024,4]{1,0:T(8,128)} async-done(((f32[2048,4]{1,0:T(8,128)}), f32[1024,4]{1,0:T(8,128)}) %reduce-scatter.25.cloned.1.call-update) | async-done | bytes 16400
  878.2 10.1 all_to_all.103
  888.3 11.9 %reduce-scatter.17.cloned.1.call-done = bf16[1024,256]{1,0:T(8,128)(2,1)} async-done(((bf16[2048,256]{1,0:T(8,128)(2,1)}), bf16[1024,256]{1,0:T(8,128)(2,1)}) %reduce-scatter.17.cloned.1.call-update) | async-done | bytes 524304 | tf_op jit(solution)/shard_map/reduce_scatter | solution.py:238
  900.2 6.1 all-to-all-start.3
  906.8 16.5 %reduce-scatter.19.cloned.1.call-done = bf16[1024,256]{1,0:T(8,128)(2,1)} async-done(((bf16[2048,256]{1,0:T(8,128)(2,1)}), bf16[1024,256]{1,0:T(8,128)(2,1)}) %reduce-scatter.19.cloned.1.call-update) | async-done | bytes 524304 | tf_op jit(solution)/shard_map/reduce_scatter | solution.py:238
  923.3 6.1 all-to-all-start.4
  930.8 15.1 %reduce-scatter.21.cloned.1.call-done = bf16[256,1024]{1,0:T(8,128)(2,1)} async-done(((bf16[256,2048]{1,0:T(8,128)(2,1)}), bf16[256,1024]{1,0:T(8,128)(2,1)}) %reduce-scatter.21.cloned.1.call-update) | async-done | bytes 524304 | tf_op jit(solution)/shard_map/reduce_scatter | solution.py:260
  947.8 6.1 all-to-all-start.6
  954.0 5.0 all-reduce.54
  959.0 19.6 %all-gather = f32[8,1,256]{2,1,0:T(1,128)S(1)} all-gather(f32[1,1,256]{2,1,0:T(1,128)S(1)} %bitcast.647), channel_id=1, replica_groups=mesh['dp'=2,'seq'=8,'head'=2] {'seq'}, dimensions={0}, use_global_device_ids=true | all-gather | bytes 9216 | tf_op jit(solution)/shard_map/all_gather | solution.py:271
  978.6 15.3 %all-gather.1 = f32[8,1,256]{2,1,0:T(1,128)S(1)} all-gather(f32[1,1,256]{2,1,0:T(1,128)S(1)} %bitcast.646), channel_id=1, replica_groups=mesh['dp'=2,'seq'=8,'head'=2] {'seq'}, dimensions={0}, use_global_device_ids=true | all-gather | bytes 9216 | tf_op jit(solution)/shard_map/all_gather | solution.py:271
  993.8 27.9 %all_gather.54 = f32[4,2048]{1,0:T(4,128)S(1)} all-gather(f32[4,256]{1,0:T(4,128)S(1)} %get-tuple-element.164), channel_id=1, replica_groups=mesh['dp'=2,'seq'=8,'head'=2] {'seq'}, dimensions={1}, use_global_device_ids=true | all-gather | bytes 36864 | tf_op jit(solution)/shard_map/all_gather | solution.py:271
  1022.3 22.3 %all-reduce.53 = (f32[32]{0:T(128)}, f32[32]{0:T(128)}, f32[32]{0:T(128)}) all-reduce(f32[32]{0:T(128)S(1)} %dynamic-update-slice, f32[32]{0:T(128)S(1)} %dynamic-update-slice.1, f32[32]{0:T(128)S(1)} %dynamic-update-slice.2), channel_id=1, replica_groups=mesh['dp'=2,'seq'=8,'head'=2] {'seq'}, use_global_device_ids=true, to_apply=%add.49 | all-reduce | flops 96 | bytes 768
  1048.1 43.8 %all-reduce.52 = (f32[2048]{0:T(1024)}, f32[4,256]{1,0:T(4,128)}, f32[256]{0:T(256)}) all-reduce(f32[2048]{0:T(1024)S(1)} %get-tuple-element.135, f32[4,256]{1,0:T(4,128)S(1)} %pad_add_fusion.10, f32[256]{0:T(256)S(1)} %get-tuple-element.131), channel_id=1, replica_groups=mesh['dp'=2,'seq'=8,'head'=2] {'dp','seq','head'}, use_global_device_ids=true, to_apply=%region_33.34 | all-reduce | flops 3328 | bytes 26624 | tf_op jit(solution)/shard_map/psum | solution.py:272
  (421 shorter events, 82.7 us)
Async XLA Ops:
  7.2 123.8 %all-gather.11.cloned.1.call-start = ((), (), s32[]{:S(2)}) async-start(), calls=%async_computation.15 | async-start | bytes 8912896 | tf_op jit(solution)/shard_map/all_gather | solution.py:151
  11.7 29.7 %copy-start.47 = (bf16[2048,128]{1,0:T(8,128)(2,1)S(1)}, bf16[2048,128]{1,0:T(8,128)(2,1)}, u32[]{:S(2)}) copy-start(bf16[2048,128]{1,0:T(8,128)(2,1)} %param.31) | copy-start | bytes 1572868
  11.7 174.3 %all-gather.13.cloned.1.call-start = ((), (), s32[]{:S(2)}) async-start(), calls=%async_computation.16 | async-start | bytes 1572864 | tf_op jit(solution)/shard_map/all_gather | solution.py:154
  40.6 153.1 %all-gather.15.cloned.1.call-start = ((), (), s32[]{:S(2)}) async-start(), calls=%async_computation.17 | async-start | bytes 1114112 | tf_op jit(solution)/shard_map/all_gather | solution.py:166
  41.3 170.1 %all-gather.21.cloned.1.call-start = ((), (), s32[]{:S(2)}) async-start(), calls=%async_computation.20 | async-start | bytes 1572864 | tf_op jit(solution)/shard_map/all_gather | solution.py:167
  41.4 31.6 %copy-start.43 = (bf16[2,1,128,2048]{3,2,1,0:T(8,128)(2,1)S(1)}, bf16[2,1,128,2048]{3,2,1,0:T(8,128)(2,1)}, u32[]{:S(2)}) copy-start(bf16[2,1,128,2048]{3,2,1,0:T(8,128)(2,1)} %param.33) | copy-start | bytes 3145732
  42.3 31.5 %copy-start.48 = (bf16[128,2048]{1,0:T(8,128)(2,1)S(1)}, bf16[128,2048]{1,0:T(8,128)(2,1)}, u32[]{:S(2)}) copy-start(bf16[128,2048]{1,0:T(8,128)(2,1)} %param.19) | copy-start | bytes 1572868
  72.9 54.1 %copy-start.112 = (f32[32]{0:T(128)S(1)}, f32[32]{0:T(128)}, u32[]{:S(2)}) copy-start(f32[32]{0:T(128)} %param.27) | copy-start | bytes 388
  72.9 54.1 %copy-start.113 = (f32[32]{0:T(128)S(1)}, f32[32]{0:T(128)}, u32[]{:S(2)}) copy-start(f32[32]{0:T(128)} %param.29) | copy-start | bytes 388
  72.9 56.4 %copy-start.108 = (s32[2,1]{0,1:T(1,128)S(1)}, s32[2,1]{0,1:T(1,128)}, u32[]{:S(2)}) copy-start(s32[2,1]{0,1:T(1,128)} %param.32) | copy-start | bytes 28
  72.9 56.5 %copy-start.104 = (f32[4,256]{1,0:T(4,128)S(1)}, f32[4,256]{1,0:T(4,128)}, u32[]{:S(2)}) copy-start(f32[4,256]{1,0:T(4,128)} %param.25) | copy-start | bytes 12292
  72.9 215.4 %all-gather.19.cloned.1.call-start = ((), (), s32[]{:S(2)}) async-start(), calls=%async_computation.19 | async-start | bytes 8912896 | tf_op jit(solution)/shard_map/all_gather | solution.py:168
  74.9 55.0 %all-to-all-start.1 = ((bf16[128,8,256]{0,2,1:T(8,128)(2,1)}), bf16[128,8,256]{0,2,1:T(8,128)(2,1)S(1)}, u32[]{:S(2)}, u32[]{:S(2)}) async-start(bf16[128,8,256]{0,2,1:T(8,128)(2,1)} %bitcast.42), calls=%async_computation.1 | async-start | bytes 1048576 | tf_op jit(solution)/shard_map/all_to_all | solution.py:155
  82.3 228.2 %all-gather.17.cloned.1.call-start = ((), (), s32[]{:S(2)}) async-start(), calls=%async_computation.18 | async-start | bytes 1572864 | tf_op jit(solution)/shard_map/all_gather | solution.py:154
  82.4 54.3 %copy-start.100 = (f32[4]{0:T(128)}, f32[4]{0:T(128)S(1)}, u32[]{:S(2)}) copy-start(f32[4]{0:T(128)S(1)} %fusion.174) | copy-start | bytes 52
  83.3 238.5 %copy-start.81 = (f32[1,256]{1,0:T(1,128)}, f32[1,256]{1,0:T(1,128)S(1)}, u32[]{:S(2)}) copy-start(f32[1,256]{1,0:T(1,128)S(1)} %get-tuple-element.238) | copy-start | bytes 3076
  83.3 238.5 %copy-start.83 = (f32[1,256]{1,0:T(1,128)}, f32[1,256]{1,0:T(1,128)S(1)}, u32[]{:S(2)}) copy-start(f32[1,256]{1,0:T(1,128)S(1)} %get-tuple-element.239) | copy-start | bytes 3076
  83.3 238.5 %copy-start.85 = (f32[1,256]{1,0:T(1,128)}, f32[1,256]{1,0:T(1,128)S(1)}, u32[]{:S(2)}) copy-start(f32[1,256]{1,0:T(1,128)S(1)} %get-tuple-element.240) | copy-start | bytes 3076
  83.3 238.5 %copy-start.87 = (f32[1,256]{1,0:T(1,128)}, f32[1,256]{1,0:T(1,128)S(1)}, u32[]{:S(2)}) copy-start(f32[1,256]{1,0:T(1,128)S(1)} %get-tuple-element.241) | copy-start | bytes 3076
  127.1 229.9 %copy-start.115 = (f32[4]{0:T(128)}, f32[4]{0:T(128)S(1)}, u32[]{:S(2)}) copy-start(f32[4]{0:T(128)S(1)} %dynamic_slice.33) | copy-start | bytes 52
  129.4 70.3 %copy-start.67 = (pred[2,8,128]{2,1,0:T(8,128)(4,1)}, pred[2,8,128]{2,1,0:T(8,128)(4,1)S(1)}, u32[]{:S(2)}) copy-start(pred[2,8,128]{2,1,0:T(8,128)(4,1)S(1)} %broadcast_compare_fusion.2) | copy-start | bytes 6148
  129.4 209.3 %copy-start.89 = (f32[1,256]{1,0:T(1,128)}, f32[1,256]{1,0:T(1,128)S(1)}, u32[]{:S(2)}) copy-start(f32[1,256]{1,0:T(1,128)S(1)} %get-tuple-element.247) | copy-start | bytes 3076
  129.4 209.3 %copy-start.91 = (f32[1,256]{1,0:T(1,128)}, f32[1,256]{1,0:T(1,128)S(1)}, u32[]{:S(2)}) copy-start(f32[1,256]{1,0:T(1,128)S(1)} %get-tuple-element.248) | copy-start | bytes 3076
  129.4 209.3 %copy-start.93 = (f32[1,256]{1,0:T(1,128)}, f32[1,256]{1,0:T(1,128)S(1)}, u32[]{:S(2)}) copy-start(f32[1,256]{1,0:T(1,128)S(1)} %get-tuple-element.249) | copy-start | bytes 3076
  129.4 209.3 %copy-start.95 = (f32[1,256]{1,0:T(1,128)}, f32[1,256]{1,0:T(1,128)S(1)}, u32[]{:S(2)}) copy-start(f32[1,256]{1,0:T(1,128)S(1)} %get-tuple-element.250) | copy-start | bytes 3076
  129.7 227.4 %copy-start.55 = (pred[8,128,128]{2,1,0:T(8,128)(4,1)}, pred[8,128,128]{2,1,0:T(8,128)(4,1)S(1)}, u32[]{:S(2)}) copy-start(pred[8,128,128]{2,1,0:T(8,128)(4,1)S(1)} %get-tuple-element.245) | copy-start | bytes 393220
  129.8 227.2 %copy-start.50 = (pred[2,8,128,128]{3,2,1,0:T(8,128)(4,1)}, pred[2,8,128,128]{3,2,1,0:T(8,128)(4,1)S(1)}, u32[]{:S(2)}) copy-start(pred[2,8,128,128]{3,2,1,0:T(8,128)(4,1)S(1)} %broadcast_and_fusion) | copy-start | bytes 786436
  130.9 507.0 %reduce-scatter.15.cloned.1.call-start = ((), (), s32[]{:S(2)}) async-start(), calls=%async_computation.24 | async-start | bytes 2228224 | tf_op jit(solution)/shard_map/reduce_scatter | solution.py:218
  185.9 171.2 %copy-start.71 = (f32[2,8,128,4]{2,3,1,0:T(4,128)}, f32[2,8,128,4]{2,3,1,0:T(4,128)S(1)}, u32[]{:S(2)}) copy-start(f32[2,8,128,4]{2,3,1,0:T(4,128)S(1)} %copy.554) | copy-start | bytes 98308
  199.8 147.2 %copy-start.59 = (f32[2,8,128,4]{2,3,1,0:T(4,128)}, f32[2,8,128,4]{2,3,1,0:T(4,128)S(1)}, u32[]{:S(2)}) copy-start(f32[2,8,128,4]{2,3,1,0:T(4,128)S(1)} %copy.575) | copy-start | bytes 98308
  200.1 138.7 %copy-start = (f32[8,2,128,256]{3,2,0,1:T(8,128)}, f32[8,2,128,256]{3,2,0,1:T(8,128)S(1)}, u32[]{:S(2)}) copy-start(f32[8,2,128,256]{3,2,0,1:T(8,128)S(1)} %copy.552) | copy-start | bytes 6291460
  298.7 47.0 %copy-start.76 = (f32[2,4]{1,0:T(2,128)}, f32[2,4]{1,0:T(2,128)S(1)}, u32[]{:S(2)}) copy-start(f32[2,4]{1,0:T(2,128)S(1)} %get-tuple-element.150) | copy-start | bytes 100
  298.8 50.5 %copy-start.63 = (f32[2,4]{1,0:T(2,128)}, f32[2,4]{1,0:T(2,128)S(1)}, u32[]{:S(2)}) copy-start(f32[2,4]{1,0:T(2,128)S(1)} %get-tuple-element.154) | copy-start | bytes 100
  298.8 50.5 %copy-start.65 = (f32[2,4]{1,0:T(2,128)}, f32[2,4]{1,0:T(2,128)S(1)}, u32[]{:S(2)}) copy-start(f32[2,4]{1,0:T(2,128)S(1)} %get-tuple-element.157) | copy-start | bytes 100
  298.8 51.0 %copy-start.74 = (f32[2,4]{1,0:T(2,128)}, f32[2,4]{1,0:T(2,128)S(1)}, u32[]{:S(2)}) copy-start(f32[2,4]{1,0:T(2,128)S(1)} %get-tuple-element.151) | copy-start | bytes 100
  341.6 13.2 %copy-start.3 = (f32[2,1024,128]{2,1,0:T(8,128)}, f32[2,1024,128]{2,1,0:T(8,128)S(1)}, u32[]{:S(2)}) copy-start(f32[2,1024,128]{2,1,0:T(8,128)S(1)} %get-tuple-element.221) | copy-start | bytes 3145732
  354.7 13.1 %copy-start.27 = (f32[2,8,128,4,64]{2,4,3,1,0:T(8,128)}, f32[2,8,128,4,64]{2,4,3,1,0:T(8,128)S(1)}, u32[]{:S(2)}) copy-start(f32[2,8,128,4,64]{2,4,3,1,0:T(8,128)S(1)} %fusion.55) | copy-start | bytes 6291460
  455.6 12.5 %copy-start.20 = (f32[2,8,4,64,128]{4,3,2,0,1:T(8,128)S(1)}, f32[2,8,4,64,128]{4,3,2,0,1:T(8,128)}, u32[]{:S(2)}) copy-start(f32[2,8,4,64,128]{4,3,2,0,1:T(8,128)} %copy-done.19) | copy-start | bytes 6291460
  479.1 11.9 %copy-start.68 = (pred[2,8,128]{2,1,0:T(8,128)(4,1)S(1)}, pred[2,8,128]{2,1,0:T(8,128)(4,1)}, u32[]{:S(2)}) copy-start(pred[2,8,128]{2,1,0:T(8,128)(4,1)} %copy-done.67) | copy-start | bytes 6148
  492.0 48.1 %copy-start.53 = (f32[2,8,128,4]{2,3,1,0:T(4,128)S(1)}, f32[2,8,128,4]{2,3,1,0:T(4,128)}, u32[]{:S(2)}) copy-start(f32[2,8,128,4]{2,3,1,0:T(4,128)} %get-tuple-element.137) | copy-start | bytes 98308
  492.0 48.1 %copy-start.101 = (f32[4]{0:T(128)S(1)}, f32[4]{0:T(128)}, u32[]{:S(2)}) copy-start(f32[4]{0:T(128)} %copy-done.100) | copy-start | bytes 52
  492.0 48.1 %copy-start.103 = (f32[4]{0:T(128)S(1)}, f32[4]{0:T(128)}, u32[]{:S(2)}) copy-start(f32[4]{0:T(128)} %copy-done.102) | copy-start | bytes 52
  566.6 179.7 %reduce-scatter.13.cloned.1.call-start = ((), (), s32[]{:S(2)}) async-start(), calls=%async_computation.23 | async-start | bytes 8912896 | tf_op jit(solution)/shard_map/reduce_scatter | solution.py:229
  602.5 252.8 %reduce-scatter.11.cloned.1.call-start = ((), (), s32[]{:S(2)}) async-start(), calls=%async_computation.21 | async-start | bytes 8912896 | tf_op jit(solution)/shard_map/reduce_scatter | solution.py:205
  609.6 267.4 %reduce-scatter.25.cloned.1.call-start = ((), (), s32[]{:S(2)}) async-start(), calls=%async_computation.31 | async-start | bytes 1572864
  616.6 283.6 %reduce-scatter.17.cloned.1.call-start = ((), (), s32[]{:S(2)}) async-start(), calls=%async_computation.26 | async-start | bytes 1572864 | tf_op jit(solution)/shard_map/reduce_scatter | solution.py:238
  623.8 299.5 %reduce-scatter.19.cloned.1.call-start = ((), (), s32[]{:S(2)}) async-start(), calls=%async_computation.27 | async-start | bytes 1572864 | tf_op jit(solution)/shard_map/reduce_scatter | solution.py:238
  630.9 315.0 %reduce-scatter.21.cloned.1.call-start = ((), (), s32[]{:S(2)}) async-start(), calls=%async_computation.28 | async-start | bytes 1572864 | tf_op jit(solution)/shard_map/reduce_scatter | solution.py:260
  637.8 108.4 %copy-start.31 = (bf16[2,1,128,2048]{3,2,1,0:T(8,128)(2,1)S(1)}, bf16[2,1,128,2048]{3,2,1,0:T(8,128)(2,1)}, u32[]{:S(2)}) copy-start(bf16[2,1,128,2048]{3,2,1,0:T(8,128)(2,1)} %param.17) | copy-start | bytes 3145732
  637.8 108.4 %copy-start.62 = (f32[2048]{0:T(1024)S(1)}, f32[2048]{0:T(1024)}, u32[]{:S(2)}) copy-start(f32[2048]{0:T(1024)} %param.18) | copy-start | bytes 24580
  637.9 108.4 %copy-start.99 = (f32[128]{0:T(128)S(1)}, f32[128]{0:T(128)}, u32[]{:S(2)}) copy-start(f32[128]{0:T(128)} %copy-done.98) | copy-start | bytes 1540
  637.9 406.8 %reduce-scatter.23.cloned.1.call-start = ((), (), s32[]{:S(2)}) async-start(), calls=%async_computation.29 | async-start | bytes 2228224 | tf_op jit(solution)/shard_map/reduce_scatter | solution.py:253
  638.0 108.3 %copy-start.49 = (f32[128,256]{1,0:T(8,128)S(1)}, f32[128,256]{1,0:T(8,128)}, u32[]{:S(2)}) copy-start(f32[128,256]{1,0:T(8,128)} %reduce-scatter.15.cloned.1.call-done) | copy-start | bytes 393220
  640.7 107.5 %copy-start.111 = (f32[128]{0:T(128)S(1)}, f32[128]{0:T(128)}, u32[]{:S(2)}) copy-start(f32[128]{0:T(128)} %copy-done.110) | copy-start | bytes 1540
  640.8 214.5 %copy-start.44 = (bf16[2,1,128,2048]{3,2,1,0:T(8,128)(2,1)S(1)}, bf16[2,1,128,2048]{3,2,1,0:T(8,128)(2,1)}, u32[]{:S(2)}) copy-start(bf16[2,1,128,2048]{3,2,1,0:T(8,128)(2,1)} %param.33) | copy-start | bytes 3145732
  640.8 451.1 %all-gather.23.cloned.1.call-start = ((), (), s32[]{:S(2)}) async-start(), calls=%async_computation.22 | async-start | bytes 1572864 | tf_op jit(solution)/shard_map/all_gather | solution.py:268
  857.9 71.5 %copy-start.114 = (u32[32]{0:T(128)S(1)}, u32[32]{0:T(128)}, u32[]{:S(2)}) copy-start(u32[32]{0:T(128)} %constant.176) | copy-start | bytes 388
  900.2 23.1 %all-to-all-start.3 = ((bf16[8,128,256]{2,1,0:T(8,128)(2,1)}), bf16[8,128,256]{2,1,0:T(8,128)(2,1)S(1)}, u32[]{:S(2)}, u32[]{:S(2)}) async-start(bf16[8,128,256]{2,1,0:T(8,128)(2,1)} %bitcast.598), calls=%async_computation.7 | async-start | bytes 1048576 | tf_op jit(solution)/shard_map/all_to_all | solution.py:237
  906.2 185.7 %all-gather.25.cloned.1.call-start = ((), (), s32[]{:S(2)}) async-start(), calls=%async_computation.25 | async-start | bytes 3145728 | tf_op jit(solution)/shard_map/all_gather | solution.py:268
  906.2 47.7 %copy-start.107 = (f32[32]{0:T(128)S(1)}, f32[32]{0:T(128)}, u32[]{:S(2)}) copy-start(f32[32]{0:T(128)} %param.28) | copy-start | bytes 388
  906.2 47.7 %copy-start.109 = (f32[4]{0:T(128)S(1)}, f32[4]{0:T(128)}, u32[]{:S(2)}) copy-start(f32[4]{0:T(128)} %get-tuple-element.130) | copy-start | bytes 52
  923.3 24.5 %all-to-all-start.4 = ((bf16[8,128,256]{2,1,0:T(8,128)(2,1)}), bf16[8,128,256]{2,1,0:T(8,128)(2,1)S(1)}, u32[]{:S(2)}, u32[]{:S(2)}) async-start(bf16[8,128,256]{2,1,0:T(8,128)(2,1)} %bitcast.597), calls=%async_computation.9 | async-start | bytes 1048576 | tf_op jit(solution)/shard_map/all_to_all | solution.py:237
  947.8 99.2 %all-to-all-start.6 = ((bf16[256,8,128]{2,0,1:T(8,128)(2,1)}), bf16[256,8,128]{2,0,1:T(8,128)(2,1)S(1)}, u32[]{:S(2)}, u32[]{:S(2)}) async-start(bf16[256,8,128]{2,0,1:T(8,128)(2,1)} %copy_bitcast_fusion), calls=%async_computation.12 | async-start | bytes 1048576 | tf_op jit(solution)/shard_map/all_to_all | solution.py:259
  953.9 138.0 %all-reduce.57.cloned.1.call-start = ((), (), s32[]{:S(2)}) async-start(), calls=%async_computation.30 | async-start | bytes 262144 | tf_op jit(solution)/shard_map/psum | solution.py:254
  (74 other events, 292.6 us)
Sparse Core Ops, SparseCore 0:
  11.8 93.3 all-gather.10
  107.3 24.0 all-gather.12
  134.2 54.7 all-gather.14
  190.5 20.8 all-gather.20
  214.0 74.2 all-gather.18
  290.3 20.1 all-gather.16
  566.6 70.9 reduce-scatter.14
  642.2 103.9 reduce-scatter.12
  750.8 104.4 reduce-scatter.10
  858.0 18.9 reduce-scatter.24
  879.8 20.3 reduce-scatter.16
  902.9 20.3 reduce-scatter.18
  925.5 20.3 reduce-scatter.20
  948.7 76.7 reduce-scatter.22
  1026.9 14.2 all-gather.22
  1043.2 11.7 all-gather.24
  1057.3 19.0 all-reduce.56
